TPU v7x, 32 devices: a whole 2x2x4 slice. The times are simulated.
32 devices in a mesh: design: 2 (over y), space: 8 (over z, x), case: 2 (over core).
Axes of the slice: x: 2, y: 2, z: 4, core: 2. Of those that a mesh axis runs over, the one named last changes fastest.
Arguments:
- displacement: float32 [16, 3, 96, 16, 128], P(('design', 'case'), None, 'space'), parts along dimension 0, may hold values from -3 to 3
- forces: float32 [16, 3, 96, 16, 128], P(('design', 'case'), None, 'space'), parts along dimension 0, may hold values from -13.6 to 13.6
- density: float32 [192, 16, 128], P(('design', 'space')), parts along dimension 0, may hold values from 0.1 to 1
- support_mask: int32 [192, 16, 128], P(('design', 'space')), parts along dimension 0, may hold values 0 or 1
- void_mask: int32 [192, 16, 128], P(('design', 'space')), parts along dimension 0, may hold values 0 or 1
Outputs:
- smoothed: float32 [16, 3, 96, 16, 128], P(('design', 'case'), None, 'space'), parts along dimension 0
- new_density: float32 [192, 16, 128], P(('design', 'space')), parts along dimension 0
- ks_value: float32 [2], P('design'), parts along dimension 0
There are 2 independent parts, one for each index of `design`. A program takes and returns all parts, laid end to end along the dimension named above; each array names one. Nothing has to cross between parts.
All inputs are finite; a program needn't handle non-finite values. No bound on the sum of `support_mask` or of `void_mask` on one device may be relied on, other than what follows from the above.
Results may differ from a plain program's by a relative error of at most 0.00002.
Values sent between devices are 32-bit elements; how exact they have to be, the bound alone decides.
A program may use at most 64 MiB of HBM per device.

v0:
```python
import math
import jax
import jax.numpy as jnp
from jax import lax
from jax.sharding import PartitionSpec as P

STIFF_MIN = 0.001
DIAG_SHIFT = 0.5
KS_BETA = 8.0
MOVE_LIMIT = 0.2
DENSITY_MIN = 0.001
STEP_ONE = 1.0 / (1.15 + 0.85 * math.cos(math.pi / 4))
STEP_TWO = 1.0 / (1.15 - 0.85 * math.cos(math.pi / 4))


def with_halo(block, sides, width):
    for axis, dim in sides:
        count = lax.axis_size(axis)
        forward = [(i, i + 1) for i in range(count - 1)]
        backward = [(target, source) for source, target in forward]
        low = lax.ppermute(
            lax.slice_in_dim(block, block.shape[dim] - width, None, axis=dim), axis, forward
        )
        high = lax.ppermute(lax.slice_in_dim(block, 0, width, axis=dim), axis, backward)
        block = jnp.concatenate([low, block, high], axis=dim)
    return block


def pad_axis(values, axis, width):
    widths = [(0, 0)] * values.ndim
    widths[values.ndim + axis] = (width, width)
    return jnp.pad(values, widths)


def stencil(fields, cube):
    face_x = STIFF_MIN + 0.5 * (cube[:-1] + cube[1:])
    middle = cube[1:-1]
    cube_y = pad_axis(middle, -2, 1)
    face_y = STIFF_MIN + 0.5 * (cube_y[:, :-1] + cube_y[:, 1:])
    cube_z = pad_axis(middle, -1, 1)
    face_z = STIFF_MIN + 0.5 * (cube_z[:, :, :-1] + cube_z[:, :, 1:])
    centre = fields[..., 1:-1, :, :]
    padded_y = pad_axis(centre, -2, 1)
    padded_z = pad_axis(centre, -1, 1)
    fluxes = face_x[1:] * (centre - fields[..., 2:, :, :]) + face_x[:-1] * (
        centre - fields[..., :-2, :, :]
    )
    fluxes = (
        fluxes
        + face_y[:, 1:] * (centre - padded_y[..., 2:, :])
        + face_y[:, :-1] * (centre - padded_y[..., :-2, :])
    )
    fluxes = (
        fluxes
        + face_z[:, :, 1:] * (centre - padded_z[..., 2:])
        + face_z[:, :, :-1] * (centre - padded_z[..., :-2])
    )
    diagonal = (
        DIAG_SHIFT
        + face_x[1:]
        + face_x[:-1]
        + face_y[:, 1:]
        + face_y[:, :-1]
        + face_z[:, :, 1:]
        + face_z[:, :, :-1]
    )
    return (DIAG_SHIFT * centre + fluxes, diagonal)


def smooth_sweep(fields, loads, cube, keep, factor):
    applied, diagonal = stencil(fields, cube)
    centre = fields[..., 1:-1, :, :]
    return keep * (centre + factor * (loads - applied) / diagonal)


def energy(extended, density):
    centre = extended[..., 1:-1, :, :]
    padded_y = pad_axis(centre, -2, 1)
    padded_z = pad_axis(centre, -1, 1)
    squares = (centre - extended[..., 2:, :, :]) ** 2 + (centre - extended[..., :-2, :, :]) ** 2
    squares = squares + (centre - padded_y[..., 2:, :]) ** 2 + (centre - padded_y[..., :-2, :]) ** 2
    squares = squares + (centre - padded_z[..., 2:]) ** 2 + (centre - padded_z[..., :-2]) ** 2
    return -1.5 * density * density * jnp.sum(squares, axis=-4)


def face_rim(motion):
    return with_halo(motion, (("space", 2),), 1)


def body(displacement, forces, density, support_mask, void_mask):
    planes = density.shape[0]
    rows_y = density.shape[1]
    rows_z = density.shape[2]
    slab_index = lax.axis_index("space")
    total_planes = planes * lax.axis_size("space")
    cells = total_planes * rows_y * rows_z
    keep = (1 - support_mask).astype(jnp.float32)
    cube_ext = with_halo(density, (("space", 0),), 1) ** 3
    motion = smooth_sweep(face_rim(displacement), forces, cube_ext, keep, STEP_ONE)
    motion = smooth_sweep(face_rim(motion), forces, cube_ext, keep, STEP_TWO)
    extended = face_rim(motion)
    case_sens = energy(extended, density)
    local_work = jnp.sum(forces * motion, axis=(1, 2, 3, 4))
    score_scale = KS_BETA / (3.0 * cells)
    scores = score_scale * lax.psum(local_work, "space")
    highest = lax.pmax(jnp.max(scores), "case")
    exponent = jnp.exp(scores - highest)
    denominator = lax.psum(jnp.sum(exponent), "case")
    weights = exponent / denominator
    ks_value = (highest + jnp.log(denominator)) / KS_BETA
    combined = lax.psum(jnp.sum(weights[:, None, None, None] * case_sens, axis=0), "case")
    product = density * combined
    rim_rows = with_halo(product, (("space", 0),), 1)
    padded_y = pad_axis(product, -2, 1)
    padded_z = pad_axis(product, -1, 1)
    neighbours = (
        rim_rows[2:]
        + rim_rows[:-2]
        + padded_y[:, 2:]
        + padded_y[:, :-2]
        + padded_z[:, :, 2:]
        + padded_z[:, :, :-2]
    )
    plane_ids = slab_index * planes + jnp.arange(planes)
    x_count = (plane_ids > 0).astype(jnp.float32) + (plane_ids < total_planes - 1).astype(
        jnp.float32
    )
    y_ids = jnp.arange(rows_y)
    y_count = (y_ids > 0).astype(jnp.float32) + (y_ids < rows_y - 1).astype(jnp.float32)
    z_ids = jnp.arange(rows_z)
    z_count = (z_ids > 0).astype(jnp.float32) + (z_ids < rows_z - 1).astype(jnp.float32)
    counts = x_count[:, None, None] + y_count[None, :, None] + z_count[None, None, :]
    filtered = (2.0 * product + neighbours) / (density * (2.0 + counts))
    scale = lax.psum(jnp.sum(-filtered), "space") / cells + 1e-06
    updated = jnp.clip(density + MOVE_LIMIT * (-filtered / scale - 1.0), DENSITY_MIN, 1.0)
    new_density = jnp.where(void_mask == 1, DENSITY_MIN, updated)
    return (motion, new_density, ks_value.reshape(1))


def solution(mesh):
    return jax.shard_map(
        body,
        mesh=mesh,
        in_specs=(
            P(("design", "case"), None, "space", None, None),
            P(("design", "case"), None, "space", None, None),
            P(("design", "space"), None, None),
            P(("design", "space"), None, None),
            P(("design", "space"), None, None),
        ),
        out_specs=(
            P(("design", "case"), None, "space", None, None),
            P(("design", "space"), None, None),
            P("design"),
        ),
        check_vma=False,
    )
```

profile of v0, /device:TPU:0, one launch (start us, length us, event | category | flops | bytes accessed | tf_op | source)
XLA Modules:
  0.0 140.1 jit_solution(4590353172492582459)
XLA Ops:
  7.2 0.0 all-reduce.12.cloned.1.call-start
  7.2 0.7 fusion.90
  7.9 4.9 %collective-permute-start = (f32[1,16,128]{2,1,0:T(8,128)S(1)}, f32[1,16,128]{2,1,0:T(8,128)S(1)}, u32[]{:S(2)}, u32[]{:S(2)}) collective-permute-start(f32[1,16,128]{2,1,0:T(8,128)S(1)} %get-tuple-element.25), channel_id=1, source_target_pairs={{0,2},{2,4},{4,6},{6,8},{8,10},{10,12},{12,14},{1,3},{3,5},{5,7},{... | collective-permute-start | bytes 24584 | tf_op jit(solution)/shard_map/ppermute | solution.py:21
  12.8 1.3 collective-permute-start.1
  14.1 1.0 fusion.87
  15.1 1.3 collective-permute-start.2
  16.4 5.2 %collective-permute-start.3 = (f32[4,3,1,16,128]{4,3,2,1,0:T(8,128)S(1)}, f32[4,3,1,16,128]{4,3,2,1,0:T(8,128)S(1)}, u32[]{:S(2)}, u32[]{:S(2)}) collective-permute-start(f32[4,3,1,16,128]{4,3,2,1,0:T(8,128)S(1)} %get-tuple-element.12), channel_id=1, source_target_pairs={{0,2},{2,4},{4,6},{6,8},{8,10},{10,12},{12,14},{1,3},{3,5},{5,7},{... | collective-permute-start | bytes 294920 | tf_op jit(solution)/shard_map/ppermute | solution.py:21
  21.5 0.9 subtract_convert_fusion
  22.5 0.0 collective-permute-done
  22.5 0.9 multiply_multiply_fusion.1
  23.4 0.0 collective-permute-done.1
  23.4 0.0 copy-start.3
  23.4 0.0 copy-start
  23.5 0.1 fusion.66
  23.7 0.1 fusion.88
  23.8 0.0 collective-permute-done.2
  23.8 0.3 collective-permute-done.3
  24.1 0.6 copy-done.3
  24.7 0.4 copy-done
  25.0 1.5 %fusion.63 = f32[4,3,12,16,128]{4,3,2,1,0:T(8,128)S(1)} fusion(f32[4,3,12,16,128]{4,3,2,1,0:T(8,128)S(1)} %copy-done.3, f32[4,3,12,16,128]{4,3,2,1,0:T(8,128)S(1)} %copy-done, f32[4,3,1,16,128]{4,3,2,1,0:T(8,128)S(1)} %collective-permute-done.3, f32[4,3,1,16,128]{4,3,2,1,0:T(8,128)S(1)} %collective-permute-done.2, f32[12,16,128]{2,1,0:T(8,128)S(1)} %get-tuple-element.14, ...), kind=kLoop, calls=%fused_computation.82 | loop fusion | flops 7667712 | bytes 4521984 | tf_op jit(solution)/shard_map/mul | solution.py:73
  26.5 1.3 collective-permute-start.4
  27.8 6.1 %collective-permute-start.5 = (f32[4,3,1,16,128]{4,3,2,1,0:T(8,128)S(1)}, f32[4,3,1,16,128]{4,3,2,1,0:T(8,128)}, u32[]{:S(2)}, u32[]{:S(2)}) collective-permute-start(f32[4,3,1,16,128]{4,3,2,1,0:T(8,128)S(1)} %get-tuple-element.10), channel_id=1, source_target_pairs={{0,2},{2,4},{4,6},{6,8},{8,10},{10,12},{12,14},{1,3},{3,5},{5,7},{... | collective-permute-start | bytes 294920 | tf_op jit(solution)/shard_map/ppermute | solution.py:21
  33.9 0.0 collective-permute-done.4
  34.0 1.5 %collective-permute-done.5 = f32[4,3,1,16,128]{4,3,2,1,0:T(8,128)} collective-permute-done((f32[4,3,1,16,128]{4,3,2,1,0:T(8,128)S(1)}, f32[4,3,1,16,128]{4,3,2,1,0:T(8,128)}, u32[]{:S(2)}, u32[]{:S(2)}) %collective-permute-start.5) | collective-permute-done | bytes 98336 | tf_op jit(solution)/shard_map/ppermute | solution.py:21
  35.5 2.4 %fusion.62 = f32[4,3,12,16,128]{4,3,2,1,0:T(8,128)S(1)} fusion(f32[4,3,12,16,128]{4,3,2,1,0:T(8,128)S(1)} %fusion.63, f32[4,3,12,16,128]{4,3,2,1,0:T(8,128)S(1)} %copy-done, f32[4,3,1,16,128]{4,3,2,1,0:T(8,128)} %collective-permute-done.5, f32[4,3,1,16,128]{4,3,2,1,0:T(8,128)S(1)} %collective-permute-done.4, f32[12,16,128]{2,1,0:T(8,128)S(1)} %get-tuple-element.14, ...), kind=kLoop, calls=%fused_computation.81 | loop fusion | flops 7667712 | bytes 4521984 | tf_op jit(solution)/shard_map/mul | solution.py:73
  37.9 0.0 copy-start.1
  37.9 1.3 collective-permute-start.6
  39.2 5.5 %collective-permute-start.7 = (f32[4,3,1,16,128]{4,3,2,1,0:T(8,128)S(1)}, f32[4,3,1,16,128]{4,3,2,1,0:T(8,128)S(1)}, u32[]{:S(2)}, u32[]{:S(2)}) collective-permute-start(f32[4,3,1,16,128]{4,3,2,1,0:T(8,128)S(1)} %get-tuple-element.8), channel_id=1, source_target_pairs={{0,2},{2,4},{4,6},{6,8},{8,10},{10,12},{12,14},{1,3},{3,5},{5,7},{... | collective-permute-start | bytes 294920 | tf_op jit(solution)/shard_map/ppermute | solution.py:21
  44.7 0.0 copy-start.2
  44.7 0.6 collective-permute-done.6
  45.3 2.0 %collective-permute-done.7 = f32[4,3,1,16,128]{4,3,2,1,0:T(8,128)S(1)} collective-permute-done((f32[4,3,1,16,128]{4,3,2,1,0:T(8,128)S(1)}, f32[4,3,1,16,128]{4,3,2,1,0:T(8,128)S(1)}, u32[]{:S(2)}, u32[]{:S(2)}) %collective-permute-start.7) | collective-permute-done | bytes 98336 | tf_op jit(solution)/shard_map/ppermute | solution.py:21
  47.3 1.1 multiply_reduce_fusion
  48.3 0.0 copy-done.1
  48.4 0.0 copy-start.4
  48.4 24.6 %psum.28 = f32[4]{0:T(128)S(1)} all-reduce(f32[4]{0:T(128)S(1)} %get-tuple-element.3), channel_id=1, replica_groups=mesh['design'=2,'space'=8,'case'=2] {'space'}, use_global_device_ids=true, to_apply=%region_1.2 | all-reduce | flops 4 | bytes 32 | tf_op jit(solution)/shard_map/psum | solution.py:105
  73.0 0.6 multiply_reduce_fusion.2
  73.6 3.1 %pmax.7 = f32[]{:T(128)} all-reduce(f32[]{:T(128)} %multiply_reduce_fusion.2), channel_id=1, replica_groups=mesh['design'=2,'space'=8,'case'=2] {'case'}, use_global_device_ids=true, to_apply=%region_3.4 | all-reduce | flops 1 | bytes 8 | tf_op jit(solution)/shard_map/pmax | solution.py:106
  76.7 1.3 fusion.82
  78.0 3.1 %psum.29 = f32[]{:T(128)} all-reduce(f32[]{:T(128)} %fusion.82), channel_id=1, replica_groups=mesh['design'=2,'space'=8,'case'=2] {'case'}, use_global_device_ids=true, to_apply=%region_5.6 | all-reduce | flops 1 | bytes 8 | tf_op jit(solution)/shard_map/psum | solution.py:108
  81.0 1.2 broadcast_divide_fusion
  82.2 0.7 multiply_reduce_fusion.1
  83.0 0.0 all-reduce.12.cloned.1.call-update
  83.0 0.1 broadcast_add_fusion
  83.1 15.2 %all-reduce.12.cloned.1.call-done = f32[12,16,128]{2,1,0:T(8,128)} async-done(((f32[12,16,128]{2,1,0:T(8,128)}), f32[12,16,128]{2,1,0:T(8,128)}) %all-reduce.12.cloned.1.call-update) | async-done | bytes 98320 | tf_op jit(solution)/shard_map/psum | solution.py:111
  98.3 0.0 copy-done.2
  98.3 0.9 mul.216
  99.2 1.3 collective-permute-start.8
  100.5 4.5 %collective-permute-start.9 = (f32[1,16,128]{2,1,0:T(8,128)S(1)}, f32[1,16,128]{2,1,0:T(8,128)S(1)}, u32[]{:S(2)}, u32[]{:S(2)}) collective-permute-start(f32[1,16,128]{2,1,0:T(8,128)S(1)} %get-tuple-element.21), channel_id=1, source_target_pairs={{0,2},{2,4},{4,6},{6,8},{8,10},{10,12},{12,14},{1,3},{3,5},{5,7},{... | collective-permute-start | bytes 24584 | tf_op jit(solution)/shard_map/ppermute | solution.py:21
  106.3 0.0 collective-permute-done.8
  106.3 0.1 collective-permute-done.9
  106.4 0.7 fusion.83
  107.8 23.0 %psum.31 = f32[]{:T(128)} all-reduce(f32[]{:T(128)S(6)} %neg.7), channel_id=1, replica_groups=mesh['design'=2,'space'=8,'case'=2] {'space'}, use_global_device_ids=true, to_apply=%region_10.11 | all-reduce | flops 1 | bytes 8 | tf_op jit(solution)/shard_map/psum | solution.py:134
  131.4 0.0 copy-done.4
  131.4 0.7 clamp_select_fusion
  (12 shorter events, 0.1 us)
Async XLA Ops:
  7.2 91.1 %all-reduce.12.cloned.1.call-start = ((), (), s32[]{:S(2)}) async-start(), calls=%async_computation | async-start | bytes 196608 | tf_op jit(solution)/shard_map/psum | solution.py:111
  7.9 14.5 %collective-permute-start = (f32[1,16,128]{2,1,0:T(8,128)S(1)}, f32[1,16,128]{2,1,0:T(8,128)S(1)}, u32[]{:S(2)}, u32[]{:S(2)}) collective-permute-start(f32[1,16,128]{2,1,0:T(8,128)S(1)} %get-tuple-element.25), channel_id=1, source_target_pairs={{0,2},{2,4},{4,6},{6,8},{8,10},{10,12},{12,14},{1,3},{3,5},{5,7},{... | collective-permute-start | bytes 24584 | tf_op jit(solution)/shard_map/ppermute | solution.py:21
  12.8 10.6 %collective-permute-start.1 = (f32[1,16,128]{2,1,0:T(8,128)S(1)}, f32[1,16,128]{2,1,0:T(8,128)S(1)}, u32[]{:S(2)}, u32[]{:S(2)}) collective-permute-start(f32[1,16,128]{2,1,0:T(8,128)S(1)} %get-tuple-element.24), channel_id=1, source_target_pairs={{2,0},{4,2},{6,4},{8,6},{10,8},{12,10},{14,12},{3,1},{5,3},{7,5},{... | collective-permute-start | bytes 24584 | tf_op jit(solution)/shard_map/ppermute | solution.py:24
  15.1 8.7 %collective-permute-start.2 = (f32[4,3,1,16,128]{4,3,2,1,0:T(8,128)S(1)}, f32[4,3,1,16,128]{4,3,2,1,0:T(8,128)S(1)}, u32[]{:S(2)}, u32[]{:S(2)}) collective-permute-start(f32[4,3,1,16,128]{4,3,2,1,0:T(8,128)S(1)} %get-tuple-element.11), channel_id=1, source_target_pairs={{2,0},{4,2},{6,4},{8,6},{10,8},{12,10},{14,12},{3,1},{5,3},{7,5},{... | collective-permute-start | bytes 294920 | tf_op jit(solution)/shard_map/ppermute | solution.py:24
  16.4 7.7 %collective-permute-start.3 = (f32[4,3,1,16,128]{4,3,2,1,0:T(8,128)S(1)}, f32[4,3,1,16,128]{4,3,2,1,0:T(8,128)S(1)}, u32[]{:S(2)}, u32[]{:S(2)}) collective-permute-start(f32[4,3,1,16,128]{4,3,2,1,0:T(8,128)S(1)} %get-tuple-element.12), channel_id=1, source_target_pairs={{0,2},{2,4},{4,6},{6,8},{8,10},{10,12},{12,14},{1,3},{3,5},{5,7},{... | collective-permute-start | bytes 294920 | tf_op jit(solution)/shard_map/ppermute | solution.py:21
  23.4 1.3 copy-start.3
  23.4 1.6 %copy-start = (f32[4,3,12,16,128]{4,3,2,1,0:T(8,128)S(1)}, f32[4,3,12,16,128]{4,3,2,1,0:T(8,128)}, u32[]{:S(2)}) copy-start(f32[4,3,12,16,128]{4,3,2,1,0:T(8,128)} %param.6) | copy-start | bytes 3538948
  26.5 7.4 %collective-permute-start.4 = (f32[4,3,1,16,128]{4,3,2,1,0:T(8,128)S(1)}, f32[4,3,1,16,128]{4,3,2,1,0:T(8,128)S(1)}, u32[]{:S(2)}, u32[]{:S(2)}) collective-permute-start(f32[4,3,1,16,128]{4,3,2,1,0:T(8,128)S(1)} %get-tuple-element.9), channel_id=1, source_target_pairs={{2,0},{4,2},{6,4},{8,6},{10,8},{12,10},{14,12},{3,1},{5,3},{7,5},{... | collective-permute-start | bytes 294920 | tf_op jit(solution)/shard_map/ppermute | solution.py:24
  27.8 7.6 %collective-permute-start.5 = (f32[4,3,1,16,128]{4,3,2,1,0:T(8,128)S(1)}, f32[4,3,1,16,128]{4,3,2,1,0:T(8,128)}, u32[]{:S(2)}, u32[]{:S(2)}) collective-permute-start(f32[4,3,1,16,128]{4,3,2,1,0:T(8,128)S(1)} %get-tuple-element.10), channel_id=1, source_target_pairs={{0,2},{2,4},{4,6},{6,8},{8,10},{10,12},{12,14},{1,3},{3,5},{5,7},{... | collective-permute-start | bytes 294920 | tf_op jit(solution)/shard_map/ppermute | solution.py:21
  37.9 10.5 %copy-start.1 = (f32[4,3,12,16,128]{4,3,2,1,0:T(8,128)}, f32[4,3,12,16,128]{4,3,2,1,0:T(8,128)S(1)}, u32[]{:S(2)}) copy-start(f32[4,3,12,16,128]{4,3,2,1,0:T(8,128)S(1)} %fusion.62) | copy-start | bytes 3538948
  37.9 7.4 %collective-permute-start.6 = (f32[4,3,1,16,128]{4,3,2,1,0:T(8,128)S(1)}, f32[4,3,1,16,128]{4,3,2,1,0:T(8,128)S(1)}, u32[]{:S(2)}, u32[]{:S(2)}) collective-permute-start(f32[4,3,1,16,128]{4,3,2,1,0:T(8,128)S(1)} %get-tuple-element.7), channel_id=1, source_target_pairs={{2,0},{4,2},{6,4},{8,6},{10,8},{12,10},{14,12},{3,1},{5,3},{7,5},{... | collective-permute-start | bytes 294920 | tf_op jit(solution)/shard_map/ppermute | solution.py:24
  39.2 8.1 %collective-permute-start.7 = (f32[4,3,1,16,128]{4,3,2,1,0:T(8,128)S(1)}, f32[4,3,1,16,128]{4,3,2,1,0:T(8,128)S(1)}, u32[]{:S(2)}, u32[]{:S(2)}) collective-permute-start(f32[4,3,1,16,128]{4,3,2,1,0:T(8,128)S(1)} %get-tuple-element.8), channel_id=1, source_target_pairs={{0,2},{2,4},{4,6},{6,8},{8,10},{10,12},{12,14},{1,3},{3,5},{5,7},{... | collective-permute-start | bytes 294920 | tf_op jit(solution)/shard_map/ppermute | solution.py:21
  44.7 53.6 %copy-start.2 = (f32[12,16,128]{2,1,0:T(8,128)S(1)}, f32[12,16,128]{2,1,0:T(8,128)}, u32[]{:S(2)}) copy-start(f32[12,16,128]{2,1,0:T(8,128)} %param.7) | copy-start | bytes 294916
  48.4 83.1 %copy-start.4 = (s32[12,16,128]{2,1,0:T(8,128)S(1)}, s32[12,16,128]{2,1,0:T(8,128)}, u32[]{:S(2)}) copy-start(s32[12,16,128]{2,1,0:T(8,128)} %param.9) | copy-start | bytes 294916
  99.2 7.1 %collective-permute-start.8 = (f32[1,16,128]{2,1,0:T(8,128)S(1)}, f32[1,16,128]{2,1,0:T(8,128)S(1)}, u32[]{:S(2)}, u32[]{:S(2)}) collective-permute-start(f32[1,16,128]{2,1,0:T(8,128)S(1)} %get-tuple-element.20), channel_id=1, source_target_pairs={{2,0},{4,2},{6,4},{8,6},{10,8},{12,10},{14,12},{3,1},{5,3},{7,5},{... | collective-permute-start | bytes 24584 | tf_op jit(solution)/shard_map/ppermute | solution.py:24
  100.5 5.9 %collective-permute-start.9 = (f32[1,16,128]{2,1,0:T(8,128)S(1)}, f32[1,16,128]{2,1,0:T(8,128)S(1)}, u32[]{:S(2)}, u32[]{:S(2)}) collective-permute-start(f32[1,16,128]{2,1,0:T(8,128)S(1)} %get-tuple-element.21), channel_id=1, source_target_pairs={{0,2},{2,4},{4,6},{6,8},{8,10},{10,12},{12,14},{1,3},{3,5},{5,7},{... | collective-permute-start | bytes 24584 | tf_op jit(solution)/shard_map/ppermute | solution.py:21
Sparse Core Ops, SparseCore 0:
  83.1 15.0 all-reduce.11
where the time goes:
time: 141 us; the launch traced here: 140 us
  blocking collectives  53.8 us (38%)
  starting transfers between devices  32.6 us (23%)
  waiting for transfers between devices  19.8 us (14%)
  between operations  18 us (13%)
  other arithmetic  13.2 us (9%)
  local copies, waits for them, and re-layouts  2.71 us (2%)
    ppermute x5, starting transfers between devices, with_halo(): lax.ppermute(lax.slice_in_dim(block, block.shape[dim] - width, None, axis...  26.1 us
    psum x1, blocking collectives, body(): scores = score_scale * lax.psum(local_work, 'space')  24.6 us
    psum x1, blocking collectives, body(): scale = lax.psum(jnp.sum(-filtered), 'space') / cells + 1e-06  23 us
    psum x1, waiting for transfers between devices, body(): lax.psum(jnp.sum(weights[:, None, None, None] * case_sens, axis=0), 'case')  15.2 us
    ppermute x5, starting transfers between devices, with_halo(): lax.ppermute(lax.slice_in_dim(block, 0, width, axis=dim), axis, backward)  6.46 us
    ppermute x5, waiting for transfers between devices, with_halo(): lax.ppermute(lax.slice_in_dim(block, block.shape[dim] - width, None, axis...  3.92 us
    mul x2, other arithmetic, smooth_sweep(): return keep * (centre + factor * (loads - applied) / diagonal)  3.82 us
    pmax x1, blocking collectives, body(): highest = lax.pmax(jnp.max(scores), 'case')  3.08 us
  transfers between devices with their start and end apart: 11, of which 6 were waited for; matrix products, arithmetic and copies ran while one was open for 2% of the time, Pallas kernels for 0%

commit v1 on v0

--- a/solution.py
+++ b/solution.py
@@ -108,7 +108,9 @@
     denominator = lax.psum(jnp.sum(exponent), "case")
     weights = exponent / denominator
     ks_value = (highest + jnp.log(denominator)) / KS_BETA
-    combined = lax.psum(jnp.sum(weights[:, None, None, None] * case_sens, axis=0), "case")
+    combined = jnp.sum(
+        lax.all_gather(jnp.sum(weights[:, None, None, None] * case_sens, axis=0), "case"), axis=0
+    )
     product = density * combined
     rim_rows = with_halo(product, (("space", 0),), 1)
     padded_y = pad_axis(product, -2, 1)

time: 141 us -> 110 us (0.78)
  waiting for transfers between devices: 19.8 us -> 4.53 us
  between operations: 18 us -> 4.73 us
    psum x1 -> x0, waiting for transfers between devices: 15.2 us -> none  [body(): lax.psum(jnp.sum(weights[:, None, None, None] * case_sens, axis=0), 'case')]
    psum x1, blocking collectives: 23 us -> 19.9 us  [body(): scale = lax.psum(jnp.sum(-filtered), 'space') / cells + 1e-06]
    all_gather x0 -> x1, blocking collectives: none -> 1.95 us  [body(): lax.all_gather(jnp.sum(weights[:, None, None, None] * case_sens, axis=0),...]
  transfers between devices with their start and end apart: 11 -> 10, of which waited for: 6 -> 4; matrix products, arithmetic and copies ran while one was open for 2% -> 3% of each run, Pallas kernels for 0% -> 0%
where the time goes in v1:
time: 110 us; the launch traced here: 109 us
  blocking collectives  52.6 us (48%)
  starting transfers between devices  32.6 us (30%)
  other arithmetic  11.8 us (11%)
  between operations  4.73 us (4%)
  waiting for transfers between devices  4.53 us (4%)
  local copies, waits for them, and re-layouts  2.71 us (2%)
    ppermute x5, starting transfers between devices, with_halo(): lax.ppermute(lax.slice_in_dim(block, block.shape[dim] - width, None, axis...  26.1 us
    psum x1, blocking collectives, body(): scores = score_scale * lax.psum(local_work, 'space')  24.6 us
    psum x1, blocking collectives, body(): scale = lax.psum(jnp.sum(-filtered), 'space') / cells + 1e-06  19.9 us
    ppermute x5, starting transfers between devices, with_halo(): lax.ppermute(lax.slice_in_dim(block, 0, width, axis=dim), axis, backward)  6.46 us
    ppermute x5, waiting for transfers between devices, with_halo(): lax.ppermute(lax.slice_in_dim(block, block.shape[dim] - width, None, axis...  3.84 us
    mul x2, other arithmetic, smooth_sweep(): return keep * (centre + factor * (loads - applied) / diagonal)  3.82 us
    psum x1, blocking collectives, body(): denominator = lax.psum(jnp.sum(exponent), 'case')  3.08 us
    pmax x1, blocking collectives, body(): highest = lax.pmax(jnp.max(scores), 'case')  3.08 us
  transfers between devices with their start and end apart: 10, of which 4 were waited for; matrix products, arithmetic and copies ran while one was open for 3% of the time, Pallas kernels for 0%

profile of v1, /device:TPU:0, one launch (start us, length us, event | category | flops | bytes accessed | tf_op | source)
XLA Modules:
  0.0 108.9 jit_solution(18037301788106213618)
XLA Ops:
  0.6 0.7 fusion.90
  1.3 4.9 %collective-permute-start = (f32[1,16,128]{2,1,0:T(8,128)S(1)}, f32[1,16,128]{2,1,0:T(8,128)S(1)}, u32[]{:S(2)}, u32[]{:S(2)}) collective-permute-start(f32[1,16,128]{2,1,0:T(8,128)S(1)} %get-tuple-element.25), channel_id=1, source_target_pairs={{0,2},{2,4},{4,6},{6,8},{8,10},{10,12},{12,14},{1,3},{3,5},{5,7},{... | collective-permute-start | bytes 24584 | tf_op jit(solution)/shard_map/ppermute | solution.py:21
  6.2 1.3 %collective-permute-start.1 = (f32[1,16,128]{2,1,0:T(8,128)S(1)}, f32[1,16,128]{2,1,0:T(8,128)S(1)}, u32[]{:S(2)}, u32[]{:S(2)}) collective-permute-start(f32[1,16,128]{2,1,0:T(8,128)S(1)} %get-tuple-element.24), channel_id=1, source_target_pairs={{2,0},{4,2},{6,4},{8,6},{10,8},{12,10},{14,12},{3,1},{5,3},{7,5},{... | collective-permute-start | bytes 24584 | tf_op jit(solution)/shard_map/ppermute | solution.py:24
  7.5 1.0 fusion.87
  8.5 1.3 %collective-permute-start.2 = (f32[4,3,1,16,128]{4,3,2,1,0:T(8,128)S(1)}, f32[4,3,1,16,128]{4,3,2,1,0:T(8,128)S(1)}, u32[]{:S(2)}, u32[]{:S(2)}) collective-permute-start(f32[4,3,1,16,128]{4,3,2,1,0:T(8,128)S(1)} %get-tuple-element.11), channel_id=1, source_target_pairs={{2,0},{4,2},{6,4},{8,6},{10,8},{12,10},{14,12},{3,1},{5,3},{7,5},{... | collective-permute-start | bytes 294920 | tf_op jit(solution)/shard_map/ppermute | solution.py:24
  9.8 5.2 %collective-permute-start.3 = (f32[4,3,1,16,128]{4,3,2,1,0:T(8,128)S(1)}, f32[4,3,1,16,128]{4,3,2,1,0:T(8,128)S(1)}, u32[]{:S(2)}, u32[]{:S(2)}) collective-permute-start(f32[4,3,1,16,128]{4,3,2,1,0:T(8,128)S(1)} %get-tuple-element.12), channel_id=1, source_target_pairs={{0,2},{2,4},{4,6},{6,8},{8,10},{10,12},{12,14},{1,3},{3,5},{5,7},{... | collective-permute-start | bytes 294920 | tf_op jit(solution)/shard_map/ppermute | solution.py:21
  15.0 0.9 subtract_convert_fusion
  15.9 0.0 collective-permute-done
  15.9 0.9 multiply_multiply_fusion.1
  16.8 0.0 collective-permute-done.1
  16.8 0.0 copy-start.3
  16.9 0.0 copy-start
  16.9 0.1 fusion.66
  17.1 0.1 fusion.88
  17.2 0.0 collective-permute-done.2
  17.2 0.3 collective-permute-done.3
  17.5 0.6 copy-done.3
  18.1 0.4 copy-done
  18.5 1.5 %fusion.63 = f32[4,3,12,16,128]{4,3,2,1,0:T(8,128)S(1)} fusion(f32[4,3,12,16,128]{4,3,2,1,0:T(8,128)S(1)} %copy-done.3, f32[4,3,12,16,128]{4,3,2,1,0:T(8,128)S(1)} %copy-done, f32[4,3,1,16,128]{4,3,2,1,0:T(8,128)S(1)} %collective-permute-done.3, f32[4,3,1,16,128]{4,3,2,1,0:T(8,128)S(1)} %collective-permute-done.2, f32[12,16,128]{2,1,0:T(8,128)S(1)} %get-tuple-element.14, ...), kind=kLoop, calls=%fused_computation.82 | loop fusion | flops 7667712 | bytes 4521984 | tf_op jit(solution)/shard_map/mul | solution.py:73
  20.0 1.3 %collective-permute-start.4 = (f32[4,3,1,16,128]{4,3,2,1,0:T(8,128)S(1)}, f32[4,3,1,16,128]{4,3,2,1,0:T(8,128)S(1)}, u32[]{:S(2)}, u32[]{:S(2)}) collective-permute-start(f32[4,3,1,16,128]{4,3,2,1,0:T(8,128)S(1)} %get-tuple-element.9), channel_id=1, source_target_pairs={{2,0},{4,2},{6,4},{8,6},{10,8},{12,10},{14,12},{3,1},{5,3},{7,5},{... | collective-permute-start | bytes 294920 | tf_op jit(solution)/shard_map/ppermute | solution.py:24
  21.3 6.1 %collective-permute-start.5 = (f32[4,3,1,16,128]{4,3,2,1,0:T(8,128)S(1)}, f32[4,3,1,16,128]{4,3,2,1,0:T(8,128)}, u32[]{:S(2)}, u32[]{:S(2)}) collective-permute-start(f32[4,3,1,16,128]{4,3,2,1,0:T(8,128)S(1)} %get-tuple-element.10), channel_id=1, source_target_pairs={{0,2},{2,4},{4,6},{6,8},{8,10},{10,12},{12,14},{1,3},{3,5},{5,7},{... | collective-permute-start | bytes 294920 | tf_op jit(solution)/shard_map/ppermute | solution.py:21
  27.3 0.0 collective-permute-done.4
  27.4 1.5 %collective-permute-done.5 = f32[4,3,1,16,128]{4,3,2,1,0:T(8,128)} collective-permute-done((f32[4,3,1,16,128]{4,3,2,1,0:T(8,128)S(1)}, f32[4,3,1,16,128]{4,3,2,1,0:T(8,128)}, u32[]{:S(2)}, u32[]{:S(2)}) %collective-permute-start.5) | collective-permute-done | bytes 98336 | tf_op jit(solution)/shard_map/ppermute | solution.py:21
  28.9 2.4 %fusion.62 = f32[4,3,12,16,128]{4,3,2,1,0:T(8,128)S(1)} fusion(f32[4,3,12,16,128]{4,3,2,1,0:T(8,128)S(1)} %fusion.63, f32[4,3,12,16,128]{4,3,2,1,0:T(8,128)S(1)} %copy-done, f32[4,3,1,16,128]{4,3,2,1,0:T(8,128)} %collective-permute-done.5, f32[4,3,1,16,128]{4,3,2,1,0:T(8,128)S(1)} %collective-permute-done.4, f32[12,16,128]{2,1,0:T(8,128)S(1)} %get-tuple-element.14, ...), kind=kLoop, calls=%fused_computation.81 | loop fusion | flops 7667712 | bytes 4521984 | tf_op jit(solution)/shard_map/mul | solution.py:73
  31.3 0.0 copy-start.1
  31.3 1.3 %collective-permute-start.6 = (f32[4,3,1,16,128]{4,3,2,1,0:T(8,128)S(1)}, f32[4,3,1,16,128]{4,3,2,1,0:T(8,128)S(1)}, u32[]{:S(2)}, u32[]{:S(2)}) collective-permute-start(f32[4,3,1,16,128]{4,3,2,1,0:T(8,128)S(1)} %get-tuple-element.7), channel_id=1, source_target_pairs={{2,0},{4,2},{6,4},{8,6},{10,8},{12,10},{14,12},{3,1},{5,3},{7,5},{... | collective-permute-start | bytes 294920 | tf_op jit(solution)/shard_map/ppermute | solution.py:24
  32.6 5.5 %collective-permute-start.7 = (f32[4,3,1,16,128]{4,3,2,1,0:T(8,128)S(1)}, f32[4,3,1,16,128]{4,3,2,1,0:T(8,128)S(1)}, u32[]{:S(2)}, u32[]{:S(2)}) collective-permute-start(f32[4,3,1,16,128]{4,3,2,1,0:T(8,128)S(1)} %get-tuple-element.8), channel_id=1, source_target_pairs={{0,2},{2,4},{4,6},{6,8},{8,10},{10,12},{12,14},{1,3},{3,5},{5,7},{... | collective-permute-start | bytes 294920 | tf_op jit(solution)/shard_map/ppermute | solution.py:21
  38.1 0.6 collective-permute-done.6
  38.7 2.0 %collective-permute-done.7 = f32[4,3,1,16,128]{4,3,2,1,0:T(8,128)S(1)} collective-permute-done((f32[4,3,1,16,128]{4,3,2,1,0:T(8,128)S(1)}, f32[4,3,1,16,128]{4,3,2,1,0:T(8,128)S(1)}, u32[]{:S(2)}, u32[]{:S(2)}) %collective-permute-start.7) | collective-permute-done | bytes 98336 | tf_op jit(solution)/shard_map/ppermute | solution.py:21
  40.7 1.1 multiply_reduce_fusion
  41.8 0.0 copy-done.1
  41.8 0.0 copy-start.2
  41.8 0.0 copy-start.4
  41.8 24.6 %psum.21 = f32[4]{0:T(128)S(1)} all-reduce(f32[4]{0:T(128)S(1)} %get-tuple-element.3), channel_id=1, replica_groups=mesh['design'=2,'space'=8,'case'=2] {'space'}, use_global_device_ids=true, to_apply=%region_1.2 | all-reduce | flops 4 | bytes 32 | tf_op jit(solution)/shard_map/psum | solution.py:105
  66.5 0.6 multiply_reduce_fusion.2
  67.1 3.1 %pmax.7 = f32[]{:T(128)} all-reduce(f32[]{:T(128)} %multiply_reduce_fusion.2), channel_id=1, replica_groups=mesh['design'=2,'space'=8,'case'=2] {'case'}, use_global_device_ids=true, to_apply=%region_3.4 | all-reduce | flops 1 | bytes 8 | tf_op jit(solution)/shard_map/pmax | solution.py:106
  70.1 1.3 %fusion.82 = f32[]{:T(128)} fusion(f32[]{:T(128)} %pmax.7, f32[4]{0:T(128)S(1)} %psum.21), kind=kLoop, calls=%fused_computation.131 | loop fusion | flops 11 | bytes 24 | tf_op jit(solution)/shard_map/reduce_sum | solution.py:108
  71.4 0.1 broadcast_add_fusion
  71.5 3.1 %psum.22 = f32[]{:T(128)} all-reduce(f32[]{:T(128)} %fusion.82), channel_id=1, replica_groups=mesh['design'=2,'space'=8,'case'=2] {'case'}, use_global_device_ids=true, to_apply=%region_5.6 | all-reduce | flops 1 | bytes 8 | tf_op jit(solution)/shard_map/psum | solution.py:108
  74.5 1.3 %broadcast_divide_fusion = f32[4]{0:T(128)S(1)} fusion(f32[]{:T(128)} %psum.22, f32[]{:T(128)} %pmax.7, f32[4]{0:T(128)S(1)} %psum.21), kind=kLoop, calls=%fused_computation.130 | loop fusion | flops 12 | bytes 40 | tf_op jit(solution)/shard_map/div | solution.py:109
  75.8 0.1 multiply_reduce_fusion.1
  75.9 1.9 %all-gather = f32[24,16,128]{2,1,0:T(8,128)S(1)} all-gather(f32[12,16,128]{2,1,0:T(8,128)S(1)} %multiply_reduce_fusion.1), channel_id=2, replica_groups=mesh['design'=2,'space'=8,'case'=2] {'case'}, dimensions={0}, use_global_device_ids=true | all-gather | bytes 294912 | tf_op jit(solution)/shard_map/all_gather | solution.py:112
  77.9 0.0 copy-done.2
  78.0 1.3 %collective-permute-start.8 = (f32[1,16,128]{2,1,0:T(8,128)S(1)}, f32[1,16,128]{2,1,0:T(8,128)S(1)}, u32[]{:S(2)}, u32[]{:S(2)}) collective-permute-start(f32[1,16,128]{2,1,0:T(8,128)S(1)} %get-tuple-element.20), channel_id=1, source_target_pairs={{2,0},{4,2},{6,4},{8,6},{10,8},{12,10},{14,12},{3,1},{5,3},{7,5},{... | collective-permute-start | bytes 24584 | tf_op jit(solution)/shard_map/ppermute | solution.py:24
  79.3 4.5 %collective-permute-start.9 = (f32[1,16,128]{2,1,0:T(8,128)S(1)}, f32[1,16,128]{2,1,0:T(8,128)S(1)}, u32[]{:S(2)}, u32[]{:S(2)}) collective-permute-start(f32[1,16,128]{2,1,0:T(8,128)S(1)} %get-tuple-element.21), channel_id=1, source_target_pairs={{0,2},{2,4},{4,6},{6,8},{8,10},{10,12},{12,14},{1,3},{3,5},{5,7},{... | collective-permute-start | bytes 24584 | tf_op jit(solution)/shard_map/ppermute | solution.py:21
  85.2 0.0 collective-permute-done.8
  85.2 0.0 collective-permute-done.9
  85.2 0.7 fusion.83
  86.6 19.9 %psum.23 = f32[]{:T(128)} all-reduce(f32[]{:T(128)S(6)} %neg.7), channel_id=1, replica_groups=mesh['design'=2,'space'=8,'case'=2] {'space'}, use_global_device_ids=true, to_apply=%region_10.11 | all-reduce | flops 1 | bytes 8 | tf_op jit(solution)/shard_map/psum | solution.py:136
  107.1 0.0 copy-done.4
  107.1 0.7 clamp_select_fusion
  (14 shorter events, 0.1 us)
Async XLA Ops:
  1.3 14.5 %collective-permute-start = (f32[1,16,128]{2,1,0:T(8,128)S(1)}, f32[1,16,128]{2,1,0:T(8,128)S(1)}, u32[]{:S(2)}, u32[]{:S(2)}) collective-permute-start(f32[1,16,128]{2,1,0:T(8,128)S(1)} %get-tuple-element.25), channel_id=1, source_target_pairs={{0,2},{2,4},{4,6},{6,8},{8,10},{10,12},{12,14},{1,3},{3,5},{5,7},{... | collective-permute-start | bytes 24584 | tf_op jit(solution)/shard_map/ppermute | solution.py:21
  6.2 10.6 %collective-permute-start.1 = (f32[1,16,128]{2,1,0:T(8,128)S(1)}, f32[1,16,128]{2,1,0:T(8,128)S(1)}, u32[]{:S(2)}, u32[]{:S(2)}) collective-permute-start(f32[1,16,128]{2,1,0:T(8,128)S(1)} %get-tuple-element.24), channel_id=1, source_target_pairs={{2,0},{4,2},{6,4},{8,6},{10,8},{12,10},{14,12},{3,1},{5,3},{7,5},{... | collective-permute-start | bytes 24584 | tf_op jit(solution)/shard_map/ppermute | solution.py:24
  8.5 8.7 %collective-permute-start.2 = (f32[4,3,1,16,128]{4,3,2,1,0:T(8,128)S(1)}, f32[4,3,1,16,128]{4,3,2,1,0:T(8,128)S(1)}, u32[]{:S(2)}, u32[]{:S(2)}) collective-permute-start(f32[4,3,1,16,128]{4,3,2,1,0:T(8,128)S(1)} %get-tuple-element.11), channel_id=1, source_target_pairs={{2,0},{4,2},{6,4},{8,6},{10,8},{12,10},{14,12},{3,1},{5,3},{7,5},{... | collective-permute-start | bytes 294920 | tf_op jit(solution)/shard_map/ppermute | solution.py:24
  9.8 7.7 %collective-permute-start.3 = (f32[4,3,1,16,128]{4,3,2,1,0:T(8,128)S(1)}, f32[4,3,1,16,128]{4,3,2,1,0:T(8,128)S(1)}, u32[]{:S(2)}, u32[]{:S(2)}) collective-permute-start(f32[4,3,1,16,128]{4,3,2,1,0:T(8,128)S(1)} %get-tuple-element.12), channel_id=1, source_target_pairs={{0,2},{2,4},{4,6},{6,8},{8,10},{10,12},{12,14},{1,3},{3,5},{5,7},{... | collective-permute-start | bytes 294920 | tf_op jit(solution)/shard_map/ppermute | solution.py:21
  16.8 1.3 %copy-start.3 = (f32[4,3,12,16,128]{4,3,2,1,0:T(8,128)S(1)}, f32[4,3,12,16,128]{4,3,2,1,0:T(8,128)}, u32[]{:S(2)}) copy-start(f32[4,3,12,16,128]{4,3,2,1,0:T(8,128)} %param.5) | copy-start | bytes 3538948
  16.9 1.6 %copy-start = (f32[4,3,12,16,128]{4,3,2,1,0:T(8,128)S(1)}, f32[4,3,12,16,128]{4,3,2,1,0:T(8,128)}, u32[]{:S(2)}) copy-start(f32[4,3,12,16,128]{4,3,2,1,0:T(8,128)} %param.6) | copy-start | bytes 3538948
  20.0 7.4 %collective-permute-start.4 = (f32[4,3,1,16,128]{4,3,2,1,0:T(8,128)S(1)}, f32[4,3,1,16,128]{4,3,2,1,0:T(8,128)S(1)}, u32[]{:S(2)}, u32[]{:S(2)}) collective-permute-start(f32[4,3,1,16,128]{4,3,2,1,0:T(8,128)S(1)} %get-tuple-element.9), channel_id=1, source_target_pairs={{2,0},{4,2},{6,4},{8,6},{10,8},{12,10},{14,12},{3,1},{5,3},{7,5},{... | collective-permute-start | bytes 294920 | tf_op jit(solution)/shard_map/ppermute | solution.py:24
  21.3 7.6 %collective-permute-start.5 = (f32[4,3,1,16,128]{4,3,2,1,0:T(8,128)S(1)}, f32[4,3,1,16,128]{4,3,2,1,0:T(8,128)}, u32[]{:S(2)}, u32[]{:S(2)}) collective-permute-start(f32[4,3,1,16,128]{4,3,2,1,0:T(8,128)S(1)} %get-tuple-element.10), channel_id=1, source_target_pairs={{0,2},{2,4},{4,6},{6,8},{8,10},{10,12},{12,14},{1,3},{3,5},{5,7},{... | collective-permute-start | bytes 294920 | tf_op jit(solution)/shard_map/ppermute | solution.py:21
  31.3 10.5 %copy-start.1 = (f32[4,3,12,16,128]{4,3,2,1,0:T(8,128)}, f32[4,3,12,16,128]{4,3,2,1,0:T(8,128)S(1)}, u32[]{:S(2)}) copy-start(f32[4,3,12,16,128]{4,3,2,1,0:T(8,128)S(1)} %fusion.62) | copy-start | bytes 3538948
  31.3 7.4 %collective-permute-start.6 = (f32[4,3,1,16,128]{4,3,2,1,0:T(8,128)S(1)}, f32[4,3,1,16,128]{4,3,2,1,0:T(8,128)S(1)}, u32[]{:S(2)}, u32[]{:S(2)}) collective-permute-start(f32[4,3,1,16,128]{4,3,2,1,0:T(8,128)S(1)} %get-tuple-element.7), channel_id=1, source_target_pairs={{2,0},{4,2},{6,4},{8,6},{10,8},{12,10},{14,12},{3,1},{5,3},{7,5},{... | collective-permute-start | bytes 294920 | tf_op jit(solution)/shard_map/ppermute | solution.py:24
  32.6 8.1 %collective-permute-start.7 = (f32[4,3,1,16,128]{4,3,2,1,0:T(8,128)S(1)}, f32[4,3,1,16,128]{4,3,2,1,0:T(8,128)S(1)}, u32[]{:S(2)}, u32[]{:S(2)}) collective-permute-start(f32[4,3,1,16,128]{4,3,2,1,0:T(8,128)S(1)} %get-tuple-element.8), channel_id=1, source_target_pairs={{0,2},{2,4},{4,6},{6,8},{8,10},{10,12},{12,14},{1,3},{3,5},{5,7},{... | collective-permute-start | bytes 294920 | tf_op jit(solution)/shard_map/ppermute | solution.py:21
  41.8 36.1 %copy-start.2 = (f32[12,16,128]{2,1,0:T(8,128)S(1)}, f32[12,16,128]{2,1,0:T(8,128)}, u32[]{:S(2)}) copy-start(f32[12,16,128]{2,1,0:T(8,128)} %param.7) | copy-start | bytes 294916
  41.8 65.3 %copy-start.4 = (s32[12,16,128]{2,1,0:T(8,128)S(1)}, s32[12,16,128]{2,1,0:T(8,128)}, u32[]{:S(2)}) copy-start(s32[12,16,128]{2,1,0:T(8,128)} %param.9) | copy-start | bytes 294916
  78.0 7.2 %collective-permute-start.8 = (f32[1,16,128]{2,1,0:T(8,128)S(1)}, f32[1,16,128]{2,1,0:T(8,128)S(1)}, u32[]{:S(2)}, u32[]{:S(2)}) collective-permute-start(f32[1,16,128]{2,1,0:T(8,128)S(1)} %get-tuple-element.20), channel_id=1, source_target_pairs={{2,0},{4,2},{6,4},{8,6},{10,8},{12,10},{14,12},{3,1},{5,3},{7,5},{... | collective-permute-start | bytes 24584 | tf_op jit(solution)/shard_map/ppermute | solution.py:24
  79.3 5.9 %collective-permute-start.9 = (f32[1,16,128]{2,1,0:T(8,128)S(1)}, f32[1,16,128]{2,1,0:T(8,128)S(1)}, u32[]{:S(2)}, u32[]{:S(2)}) collective-permute-start(f32[1,16,128]{2,1,0:T(8,128)S(1)} %get-tuple-element.21), channel_id=1, source_target_pairs={{0,2},{2,4},{4,6},{6,8},{8,10},{10,12},{12,14},{1,3},{3,5},{5,7},{... | collective-permute-start | bytes 24584 | tf_op jit(solution)/shard_map/ppermute | solution.py:21
